TPU v7x, 512 devices: a whole 4x8x8 slice. The times are simulated.
512 devices in a mesh: dom: 64 (over z, x, core), col: 8 (over y).
Axes of the slice: x: 4, y: 8, z: 8, core: 2. Of those that a mesh axis runs over, the one named last changes fastest.
Arguments:
- feature: bfloat16 [32768, 1024], P('dom', 'col'), may hold values from -6 to 6
- cotangent: bfloat16 [32768, 1024], P('dom', 'col'), may hold values from -6 to 6
- node_type: int32 [32768], P('dom'), may hold values from 0 to 2
- self_gain: float32 [3, 1024], P(None, 'col'), may hold values from 0.1 to 1.9
- weights: bfloat16 [8, 1024, 1024], P(None, 'dom', 'col'), may hold values from -0.1875 to 0.1875
- tile_values: bfloat16 [2048, 128, 128], P('dom'), may hold values from -0.5 to 0.5
- tile_rel: int32 [2048], P('dom'), may hold values from 0 to 7
- tile_src: int32 [2048], P('dom'), may hold values from 0 to 3
- tile_peer: int32 [2048], P('dom'), may hold values from 0 to 63, as said below
- tile_count: int32 [64], P('dom'), may hold values from 24 to 32, as said below
- send_block: int32 [64, 64], P('dom'), may hold values from -1 to 3, as said below
Outputs:
- feature_grad: bfloat16 [32768, 1024], P('dom', 'col')
- weight_grad: bfloat16 [8, 1024, 1024], P(None, None, 'col')
Inputs may be any that keep to these rules, and one draw needn't show every extreme that they name: Slots 0 to tile_count - 1 of each partition hold its tiles, the others hold none; some partition uses all 32 slots in every draw. `tile_peer`: the used slots of one partition name distinct owner partitions. send_block[o, p] is at least 0 exactly when some used slot of partition p names o, and then it is that slot's destination block within o.
All inputs are finite; a program needn't handle non-finite values.
Results may differ from a plain program's by a relative error of at most 0.0052.
Values may be sent and summed in bfloat16 or wider, within the bound.
No kernel may reach another device: no remote copies, remote signals or barrier semaphores. Data moves between devices by JAX's collectives and lax.ppermute only.
A program may use at most 64 MiB of HBM per device.

v0:
```python
import math
import jax
import jax.numpy as jnp
from jax import lax
from jax.sharding import PartitionSpec as P


def body(
    feature,
    cotangent,
    node_type,
    self_gain,
    weights,
    tile_values,
    tile_rel,
    tile_src,
    tile_peer,
    tile_count,
    send_block,
):
    partitions = lax.axis_size("dom")
    row_count, col_width = cotangent.shape
    tile_size = tile_values.shape[1]
    block_count = row_count // tile_size
    relations = weights.shape[0]
    slot_count = tile_values.shape[0]
    type_count = self_gain.shape[0]
    grad_blocks = cotangent.reshape(block_count, tile_size, col_width)
    wanted = send_block[0]
    chooser = (wanted[:, None] == jnp.arange(block_count, dtype=jnp.int32)[None, :]).astype(
        jnp.bfloat16
    )
    outgoing = jnp.einsum(
        "pb,btk->ptk", chooser, grad_blocks, preferred_element_type=jnp.float32
    ).astype(jnp.bfloat16)
    incoming = lax.all_to_all(outgoing, "dom", split_axis=0, concat_axis=0, tiled=True)
    picked = jnp.take(incoming, tile_peer, axis=0)
    contribs = jnp.einsum("tds,tdk->tsk", tile_values, picked, preferred_element_type=jnp.float32)
    is_used = jnp.arange(slot_count, dtype=jnp.int32) < tile_count[0]
    slot_of = tile_rel * block_count + tile_src
    slot_table = (
        (slot_of[None, :] == jnp.arange(relations * block_count, dtype=jnp.int32)[:, None])
        & is_used[None, :]
    ).astype(jnp.float32)
    merged = jnp.einsum("mt,tsk->msk", slot_table, contribs, precision=lax.Precision.HIGHEST)
    block_grad = merged.astype(jnp.bfloat16).reshape(relations, row_count, col_width)
    kind_table = (node_type[:, None] == jnp.arange(type_count, dtype=jnp.int32)[None, :]).astype(
        jnp.float32
    )
    self_gains = jnp.dot(kind_table, self_gain, precision=lax.Precision.HIGHEST)
    self_term = cotangent.astype(jnp.float32) * self_gains
    weight_full = lax.all_gather(weights, "dom", axis=1, tiled=True)
    weight_cols = lax.all_to_all(weight_full, "col", split_axis=1, concat_axis=2, tiled=True)
    aggregated = jnp.einsum(
        "rnk,rjk->nj",
        lax.all_gather(block_grad, "col", axis=2, tiled=True),
        weight_cols,
        preferred_element_type=jnp.float32,
    )
    feature_grad = (aggregated + self_term).astype(jnp.bfloat16)
    weight_terms = jnp.einsum(
        "nj,rnk->rjk",
        lax.all_gather(feature, "col", axis=1, tiled=True),
        block_grad,
        preferred_element_type=jnp.float32,
    )
    norm_scale = 1.0 / math.sqrt(row_count * partitions)
    summed = lax.psum(weight_terms, "dom")
    weight_grad = (summed * norm_scale).astype(jnp.bfloat16)
    return (feature_grad, weight_grad)


def solution(mesh):
    return jax.shard_map(
        body,
        mesh=mesh,
        in_specs=(
            P("dom", "col"),
            P("dom", "col"),
            P("dom"),
            P(None, "col"),
            P(None, "dom", "col"),
            P("dom", None, None),
            P("dom"),
            P("dom"),
            P("dom"),
            P("dom"),
            P("dom", None),
        ),
        out_specs=(P("dom", "col"), P(None, None, "col")),
        check_vma=False,
    )
```

profile of v0, /device:TPU:2, one launch (start us, length us, event | category | flops | bytes accessed | tf_op | source)
XLA Modules:
  0.0 470.0 jit_solution(14236573666321858946)
XLA Ops:
  7.2 0.0 copy-start
  7.2 0.0 all-gather.8.cloned.1.call-start
  7.2 0.7 all-gather.8.cloned.1.call-update
  7.9 1.7 convolution_convert_fusion
  9.6 2.7 copy.38
  12.3 14.0 %all-to-all-start = ((bf16[64,128,128]{2,1,0:T(8,128)(2,1)}), bf16[64,128,128]{2,1,0:T(8,128)(2,1)S(1)}, u32[]{:S(2)}, u32[]{:S(2)}) async-start(bf16[64,128,128]{2,1,0:T(8,128)(2,1)} %copy.38), calls=%async_computation | async-start | bytes 4194304 | tf_op jit(solution)/shard_map/all_to_all | solution.py:36
  26.3 0.0 all-gather.6.cloned.1.call-start
  26.4 0.6 copy.42
  27.0 0.1 all-gather.6.cloned.1.call-update
  27.1 0.0 all-reduce.2.cloned.1.call-start
  27.8 49.7 %all-to-all-done = bf16[64,128,128]{2,1,0:T(8,128)(2,1)S(1)} async-done(((bf16[64,128,128]{2,1,0:T(8,128)(2,1)}), bf16[64,128,128]{2,1,0:T(8,128)(2,1)S(1)}, u32[]{:S(2)}, u32[]{:S(2)}) %all-to-all-start) | async-done | bytes 2097184 | tf_op jit(solution)/shard_map/all_to_all | solution.py:36
  77.6 1.7 gather_fusion
  79.3 3.1 convolution_bitcast_fusion.1
  82.4 2.4 copy.40
  84.8 1.1 convolution_convert_fusion.1
  85.9 0.4 copy.41
  86.3 0.0 all-gather.8.cloned.1.call-done
  86.4 4.8 %convolution_bitcast_fusion = f32[8,1024,128]{1,2,0:T(8,128)} fusion(bf16[8,512,128]{2,1,0:T(8,128)(2,1)S(1)} %bitcast.32, bf16[512,1024]{1,0:T(8,128)(2,1)} %all-gather.8.cloned.1.call-done), kind=kOutput, calls=%fused_computation.2 | convolution fusion | flops 1073741824 | bytes 6291456 | tf_op jit(solution)/shard_map/nj,rnk->rjk/dot_general | solution.py:61
  91.2 0.0 all-reduce.2.cloned.1.call-update
  91.2 0.0 all-gather.4.cloned.1.call-start
  91.3 0.5 all-gather.4.cloned.1.call-update
  91.8 50.8 %all-gather.6.cloned.1.call-done = bf16[8,1024,128]{2,0,1:T(8,128)(2,1)} async-done(((bf16[8,16,128]{2,0,1:T(8,128)(2,1)}), bf16[8,1024,128]{2,0,1:T(8,128)(2,1)}) %all-gather.6.cloned.1.call-update) | async-done | bytes 2097168 | tf_op jit(solution)/shard_map/all_gather | solution.py:52
  142.7 6.7 %all-to-all-start.1 = ((bf16[8,1024,128]{2,0,1:T(8,128)(2,1)}), bf16[8,1024,128]{2,0,1:T(8,128)(2,1)}, u32[]{:S(2)}, u32[]{:S(2)}) async-start(bf16[8,1024,128]{2,0,1:T(8,128)(2,1)} %all-gather.6.cloned.1.call-done), calls=%async_computation.1 | async-start | bytes 4194304 | tf_op jit(solution)/shard_map/all_to_all | solution.py:53
  149.4 202.8 %all-reduce.2.cloned.1.call-done = f32[8,1024,128]{1,2,0:T(8,128)} async-done(((f32[8,1024,128]{1,2,0:T(8,128)}), f32[8,1024,128]{1,2,0:T(8,128)}) %all-reduce.2.cloned.1.call-update) | async-done | bytes 4194320 | tf_op jit(solution)/shard_map/psum | solution.py:68
  352.2 2.8 multiply_convert_fusion
  355.0 2.4 copy.45
  357.4 0.0 all-to-all-done.1
  357.4 2.9 copy.51
  360.3 2.4 all_to_all.20
  362.7 93.4 %all-gather.4.cloned.1.call-done = bf16[8,512,1024]{2,1,0:T(8,128)(2,1)} async-done(((bf16[8,512,128]{2,1,0:T(8,128)(2,1)}), bf16[8,512,1024]{2,1,0:T(8,128)(2,1)}) %all-gather.4.cloned.1.call-update) | async-done | bytes 8388624 | tf_op jit(solution)/shard_map/all_gather | solution.py:56
  456.2 6.3 %convolution_bitcast_fusion.2 = f32[512,128]{1,0:T(8,128)S(1)} fusion(bf16[8,512,1024]{2,1,0:T(8,128)(2,1)} %all-gather.4.cloned.1.call-done, bf16[8,128,1024]{2,1,0:T(8,128)(2,1)} %all_to_all.20), kind=kOutput, calls=%fused_computation.9 | convolution fusion | flops 1073741824 | bytes 10747904 | tf_op jit(solution)/shard_map/rnk,rjk->nj/dot_general | solution.py:54
  462.5 1.0 fusion.1
  (22 shorter events, 0.1 us)
Async XLA Ops:
  7.2 72.1 %copy-start = (bf16[32,128,128]{2,1,0:T(8,128)(2,1)S(1)}, bf16[32,128,128]{2,1,0:T(8,128)(2,1)}, u32[]{:S(2)}) copy-start(bf16[32,128,128]{2,1,0:T(8,128)(2,1)} %param.16) | copy-start | bytes 3145732
  7.2 79.2 %all-gather.8.cloned.1.call-start = ((), (), s32[]{:S(2)}) async-start(), calls=%async_computation.4 | async-start | bytes 1179648 | tf_op jit(solution)/shard_map/all_gather | solution.py:63
  12.3 14.1 %copy-start.3 = (bf16[8,16,128]{2,1,0:T(8,128)(2,1)S(1)}, bf16[8,16,128]{2,1,0:T(8,128)(2,1)}, u32[]{:S(2)}) copy-start(bf16[8,16,128]{2,1,0:T(8,128)(2,1)} %param.15) | copy-start | bytes 98308
  12.3 15.5 %copy-start.6 = (s32[32]{0:T(128)S(1)}, s32[32]{0:T(128)}, u32[]{:S(2)}) copy-start(s32[32]{0:T(128)} %param.19) | copy-start | bytes 388
  12.3 15.5 %copy-start.7 = (s32[32]{0:T(128)S(1)}, s32[32]{0:T(128)}, u32[]{:S(2)}) copy-start(s32[32]{0:T(128)} %param.18) | copy-start | bytes 388
  12.3 15.5 %copy-start.8 = (s32[32]{0:T(128)S(1)}, s32[32]{0:T(128)}, u32[]{:S(2)}) copy-start(s32[32]{0:T(128)} %param.17) | copy-start | bytes 388
  12.3 65.3 %all-to-all-start = ((bf16[64,128,128]{2,1,0:T(8,128)(2,1)}), bf16[64,128,128]{2,1,0:T(8,128)(2,1)S(1)}, u32[]{:S(2)}, u32[]{:S(2)}) async-start(bf16[64,128,128]{2,1,0:T(8,128)(2,1)} %copy.38), calls=%async_computation | async-start | bytes 4194304 | tf_op jit(solution)/shard_map/all_to_all | solution.py:36
  26.3 116.4 %all-gather.6.cloned.1.call-start = ((), (), s32[]{:S(2)}) async-start(), calls=%async_computation.3 | async-start | bytes 2129920 | tf_op jit(solution)/shard_map/all_gather | solution.py:52
  27.1 325.2 %all-reduce.2.cloned.1.call-start = ((), (), s32[]{:S(2)}) async-start(), calls=%async_computation.5 | async-start | bytes 8388608 | tf_op jit(solution)/shard_map/psum | solution.py:68
  86.3 4.9 %copy-start.1 = (bf16[32,128,128]{2,1,0:T(8,128)(2,1)}, bf16[32,128,128]{2,1,0:T(8,128)(2,1)S(1)}, u32[]{:S(2)}) copy-start(bf16[32,128,128]{2,1,0:T(8,128)(2,1)S(1)} %copy.41) | copy-start | bytes 3145732
  91.2 364.9 %all-gather.4.cloned.1.call-start = ((), (), s32[]{:S(2)}) async-start(), calls=%async_computation.2 | async-start | bytes 9437184 | tf_op jit(solution)/shard_map/all_gather | solution.py:56
  142.7 214.7 %all-to-all-start.1 = ((bf16[8,1024,128]{2,0,1:T(8,128)(2,1)}), bf16[8,1024,128]{2,0,1:T(8,128)(2,1)}, u32[]{:S(2)}, u32[]{:S(2)}) async-start(bf16[8,1024,128]{2,0,1:T(8,128)(2,1)} %all-gather.6.cloned.1.call-done), calls=%async_computation.1 | async-start | bytes 4194304 | tf_op jit(solution)/shard_map/all_to_all | solution.py:53
  362.7 99.8 %copy-start.2 = (bf16[512,128]{1,0:T(8,128)(2,1)S(1)}, bf16[512,128]{1,0:T(8,128)(2,1)}, u32[]{:S(2)}) copy-start(bf16[512,128]{1,0:T(8,128)(2,1)} %param.12) | copy-start | bytes 393220
  362.7 99.8 %copy-start.4 = (f32[3,128]{1,0:T(4,128)S(1)}, f32[3,128]{1,0:T(4,128)}, u32[]{:S(2)}) copy-start(f32[3,128]{1,0:T(4,128)} %param.14) | copy-start | bytes 4612
  362.7 99.8 %copy-start.5 = (s32[512]{0:T(512)S(1)}, s32[512]{0:T(512)}, u32[]{:S(2)}) copy-start(s32[512]{0:T(512)} %param.13) | copy-start | bytes 6148
Sparse Core Ops, SparseCore 0:
  10.0 46.7 all-gather.7
  60.7 81.9 all-gather.5
  146.2 205.9 all-reduce.1
  354.3 101.8 all-gather.3
where the time goes:
time: 471 us; the launch traced here: 470 us
  waiting for transfers between devices  398 us (85%)
  starting transfers between devices  20.9 us (4%)
  matrix products  18.1 us (4%)
  local copies, waits for them, and re-layouts  15.5 us (3%)
  between operations  14.6 us (3%)
    psum x1, waiting for transfers between devices, body(): summed = lax.psum(weight_terms, 'dom')  203 us
    all_gather x1, waiting for transfers between devices, body(): lax.all_gather(block_grad, 'col', axis=2, tiled=True)  93.4 us
    all_gather x1, waiting for transfers between devices, body(): weight_full = lax.all_gather(weights, 'dom', axis=1, tiled=True)  50.8 us
    all_to_all x1, waiting for transfers between devices, body(): lax.all_to_all(outgoing, 'dom', split_axis=0, concat_axis=0, tiled=True)  49.7 us
    all_to_all x1, starting transfers between devices, body(): lax.all_to_all(outgoing, 'dom', split_axis=0, concat_axis=0, tiled=True)  14 us
  transfers between devices with their start and end apart: 6, of which 4 were waited for; matrix products, arithmetic and copies ran while one was open for 6% of the time, Pallas kernels for 0%

commit v1 on v0

--- a/solution.py
+++ b/solution.py
@@ -3,6 +3,19 @@
 import jax.numpy as jnp
 from jax import lax
 from jax.sharding import PartitionSpec as P
+
+
+def ring_gather(x, axis, dim):
+    ways = lax.axis_size(axis)
+    up = [(d, (d + 1) % ways) for d in range(ways)]
+    down = [(d, (d - 1) % ways) for d in range(ways)]
+    earlier, later = ([x], [x])
+    for _ in range(ways // 2):
+        earlier.append(lax.ppermute(earlier[-1], axis, up))
+    for _ in range((ways - 1) // 2):
+        later.append(lax.ppermute(later[-1], axis, down))
+    line = jnp.concatenate([*earlier[::-1], *later[1:]], axis=dim)
+    return jnp.roll(line, (lax.axis_index(axis) - ways // 2) * x.shape[dim], axis=dim)
 
 
 def body(
@@ -53,7 +66,7 @@
     weight_cols = lax.all_to_all(weight_full, "col", split_axis=1, concat_axis=2, tiled=True)
     aggregated = jnp.einsum(
         "rnk,rjk->nj",
-        lax.all_gather(block_grad, "col", axis=2, tiled=True),
+        ring_gather(block_grad, "col", 2),
         weight_cols,
         preferred_element_type=jnp.float32,
     )

time: 471 us -> 441 us (0.936)
  the two profiles are of different devices: /device:TPU:2 before, /device:TPU:8 now
where the time goes in v1:
time: 441 us; the launch traced here: 439 us
  waiting for transfers between devices  316 us (72%)
  starting transfers between devices  45.2 us (10%)
  local copies, waits for them, and re-layouts  43 us (10%)
  between operations  14.7 us (3%)
  matrix products  14.2 us (3%)
  other arithmetic  6.14 us (1%)
    psum x1, waiting for transfers between devices, body(): summed = lax.psum(weight_terms, 'dom')  167 us
    all_to_all x1, waiting for transfers between devices, body(): lax.all_to_all(outgoing, 'dom', split_axis=0, concat_axis=0, tiled=True)  49 us
    all_gather x1, waiting for transfers between devices, body(): lax.all_gather(feature, 'col', axis=1, tiled=True)  46 us
    ppermute x4, waiting for transfers between devices, ring_gather(): earlier.append(lax.ppermute(earlier[-1], axis, up))  43.3 us
    unnamed x27, local copies, waits for them, and re-layouts  24.5 us
    ppermute x4, starting transfers between devices, ring_gather(): earlier.append(lax.ppermute(earlier[-1], axis, up))  14.9 us
    all_to_all x1, starting transfers between devices, body(): lax.all_to_all(outgoing, 'dom', split_axis=0, concat_axis=0, tiled=True)  14.2 us
    all_gather x1, waiting for transfers between devices, body(): weight_full = lax.all_gather(weights, 'dom', axis=1, tiled=True)  10.3 us
  transfers between devices with their start and end apart: 12, of which 7 were waited for; matrix products, arithmetic and copies ran while one was open for 10% of the time, Pallas kernels for 0%

profile of v1, /device:TPU:8, one launch (start us, length us, event | category | flops | bytes accessed | tf_op | source)
XLA Modules:
  0.0 439.4 jit_solution(6450090993352072609)
XLA Ops:
  8.7 1.7 convolution_convert_fusion
  10.4 2.7 copy.38
  13.1 14.2 %all-to-all-start = ((bf16[64,128,128]{2,1,0:T(8,128)(2,1)}), bf16[64,128,128]{2,1,0:T(8,128)(2,1)}, u32[]{:S(2)}, u32[]{:S(2)}) async-start(bf16[64,128,128]{2,1,0:T(8,128)(2,1)} %copy.38), calls=%async_computation | async-start | bytes 4194304 | tf_op jit(solution)/shard_map/all_to_all | solution.py:49
  30.7 49.0 %all-to-all-done = bf16[64,128,128]{2,1,0:T(8,128)(2,1)} async-done(((bf16[64,128,128]{2,1,0:T(8,128)(2,1)}), bf16[64,128,128]{2,1,0:T(8,128)(2,1)}, u32[]{:S(2)}, u32[]{:S(2)}) %all-to-all-start) | async-done | bytes 2097184 | tf_op jit(solution)/shard_map/all_to_all | solution.py:49
  79.7 2.4 gather_fusion
  82.1 1.9 convolution_bitcast_fusion.1
  84.0 3.1 copy.40
  87.1 2.7 convolution_convert_fusion.1
  90.2 3.5 collective-permute-start
  93.8 10.3 %all-gather.3.cloned.1.call-done = bf16[8,1024,128]{2,0,1:T(8,128)(2,1)} async-done(((bf16[8,16,128]{2,0,1:T(8,128)(2,1)}), bf16[8,1024,128]{2,0,1:T(8,128)(2,1)}) %all-gather.3.cloned.1.call-update) | async-done | bytes 2097168 | tf_op jit(solution)/shard_map/all_gather | solution.py:65
  104.1 7.3 %all-to-all-start.1 = ((bf16[8,1024,128]{2,0,1:T(8,128)(2,1)}), bf16[8,1024,128]{2,0,1:T(8,128)(2,1)}, u32[]{:S(2)}, u32[]{:S(2)}) async-start(bf16[8,1024,128]{2,0,1:T(8,128)(2,1)} %all-gather.3.cloned.1.call-done), calls=%async_computation.1 | async-start | bytes 4194304 | tf_op jit(solution)/shard_map/all_to_all | solution.py:66
  111.4 15.6 %collective-permute-done = bf16[8,512,128]{2,1,0:T(8,128)(2,1)S(1)} collective-permute-done((bf16[8,512,128]{2,1,0:T(8,128)(2,1)S(1)}, bf16[8,512,128]{2,1,0:T(8,128)(2,1)S(1)}, u32[]{:S(2)}, u32[]{:S(2)}) %collective-permute-start) | collective-permute-done | bytes 1048608 | tf_op jit(solution)/shard_map/ppermute | solution.py:14
  127.0 5.3 %collective-permute-start.1 = (bf16[8,512,128]{2,1,0:T(8,128)(2,1)S(1)}, bf16[8,512,128]{2,1,0:T(8,128)(2,1)}, u32[]{:S(2)}, u32[]{:S(2)}) collective-permute-start(bf16[8,512,128]{2,1,0:T(8,128)(2,1)S(1)} %collective-permute-done), channel_id=1, source_target_pairs={{0,1},{1,2},{2,3},{3,4},{4,5},{5,6},{6,7},{7,0},{8,9},{9,10},{10,1... | collective-permute-start | bytes 3145736 | tf_op jit(solution)/shard_map/ppermute | solution.py:14
  132.2 1.9 collective-permute-start.4
  134.2 46.0 %all-gather.5.cloned.1.call-done = bf16[512,1024]{1,0:T(8,128)(2,1)} async-done(((bf16[512,128]{1,0:T(8,128)(2,1)}), bf16[512,1024]{1,0:T(8,128)(2,1)}) %all-gather.5.cloned.1.call-update) | async-done | bytes 1048592 | tf_op jit(solution)/shard_map/all_gather | solution.py:76
  180.1 4.5 %convolution_bitcast_fusion = f32[8,1024,128]{1,2,0:T(8,128)} fusion(bf16[8,512,128]{2,1,0:T(8,128)(2,1)S(1)} %bitcast.41, bf16[512,1024]{1,0:T(8,128)(2,1)} %all-gather.5.cloned.1.call-done), kind=kOutput, calls=%fused_computation.4 | convolution fusion | flops 1073741824 | bytes 6291456 | tf_op jit(solution)/shard_map/nj,rnk->rjk/dot_general | solution.py:74
  184.7 8.2 %collective-permute-done.1 = bf16[8,512,128]{2,1,0:T(8,128)(2,1)} collective-permute-done((bf16[8,512,128]{2,1,0:T(8,128)(2,1)S(1)}, bf16[8,512,128]{2,1,0:T(8,128)(2,1)}, u32[]{:S(2)}, u32[]{:S(2)}) %collective-permute-start.1) | collective-permute-done | bytes 1048608 | tf_op jit(solution)/shard_map/ppermute | solution.py:14
  192.9 3.5 collective-permute-start.2
  196.4 2.6 collective-permute-start.5
  199.0 19.5 %collective-permute-done.2 = bf16[8,512,128]{2,1,0:T(8,128)(2,1)} collective-permute-done((bf16[8,512,128]{2,1,0:T(8,128)(2,1)}, bf16[8,512,128]{2,1,0:T(8,128)(2,1)}, u32[]{:S(2)}, u32[]{:S(2)}) %collective-permute-start.2) | collective-permute-done | bytes 1048608 | tf_op jit(solution)/shard_map/ppermute | solution.py:14
  218.4 2.6 collective-permute-start.3
  221.5 4.3 collective-permute-start.6
  225.8 166.7 %all-reduce.2.cloned.1.call-done = f32[8,1024,128]{1,2,0:T(8,128)} async-done(((f32[8,1024,128]{1,2,0:T(8,128)}), f32[8,1024,128]{1,2,0:T(8,128)}) %all-reduce.2.cloned.1.call-update) | async-done | bytes 4194320 | tf_op jit(solution)/shard_map/psum | solution.py:81
  392.5 4.1 multiply_convert_fusion
  396.6 3.9 copy.45
  400.5 4.2 copy.51
  404.8 4.2 all_to_all.20
  408.9 1.7 constant_dynamic-update-slice_fusion.15
  412.2 1.6 constant_dynamic-update-slice_fusion.13
  414.6 1.6 constant_dynamic-update-slice_fusion.10
  422.6 1.6 constant_dynamic-update-slice_fusion.5
  429.8 3.1 fusion.8
  (41 shorter events, 19.3 us)
Async XLA Ops:
  7.2 74.9 %copy-start = (bf16[32,128,128]{2,1,0:T(8,128)(2,1)S(1)}, bf16[32,128,128]{2,1,0:T(8,128)(2,1)}, u32[]{:S(2)}) copy-start(bf16[32,128,128]{2,1,0:T(8,128)(2,1)} %param.16) | copy-start | bytes 3145732
  7.2 96.9 %all-gather.3.cloned.1.call-start = ((), (), s32[]{:S(2)}) async-start(), calls=%async_computation.2 | async-start | bytes 2129920 | tf_op jit(solution)/shard_map/all_gather | solution.py:65
  13.1 208.0 %copy-start.2 = (bf16[512,128]{1,0:T(8,128)(2,1)S(1)}, bf16[512,128]{1,0:T(8,128)(2,1)}, u32[]{:S(2)}) copy-start(bf16[512,128]{1,0:T(8,128)(2,1)} %param.12) | copy-start | bytes 393220
  13.1 208.0 %copy-start.3 = (f32[3,128]{1,0:T(4,128)S(1)}, f32[3,128]{1,0:T(4,128)}, u32[]{:S(2)}) copy-start(f32[3,128]{1,0:T(4,128)} %param.14) | copy-start | bytes 4612
  13.1 208.0 %copy-start.4 = (s32[512]{0:T(512)S(1)}, s32[512]{0:T(512)}, u32[]{:S(2)}) copy-start(s32[512]{0:T(512)} %param.13) | copy-start | bytes 6148
  13.1 66.6 %all-to-all-start = ((bf16[64,128,128]{2,1,0:T(8,128)(2,1)}), bf16[64,128,128]{2,1,0:T(8,128)(2,1)}, u32[]{:S(2)}, u32[]{:S(2)}) async-start(bf16[64,128,128]{2,1,0:T(8,128)(2,1)} %copy.38), calls=%async_computation | async-start | bytes 4194304 | tf_op jit(solution)/shard_map/all_to_all | solution.py:49
  27.3 152.9 %all-gather.5.cloned.1.call-start = ((), (), s32[]{:S(2)}) async-start(), calls=%async_computation.3 | async-start | bytes 1179648 | tf_op jit(solution)/shard_map/all_gather | solution.py:76
  90.2 36.7 %collective-permute-start = (bf16[8,512,128]{2,1,0:T(8,128)(2,1)S(1)}, bf16[8,512,128]{2,1,0:T(8,128)(2,1)S(1)}, u32[]{:S(2)}, u32[]{:S(2)}) collective-permute-start(bf16[8,512,128]{2,1,0:T(8,128)(2,1)S(1)} %bitcast.39), channel_id=1, source_target_pairs={{0,1},{1,2},{2,3},{3,4},{4,5},{5,6},{6,7},{7,0},{8,9},{9,10},{10,1... | collective-permute-start | bytes 3145736 | tf_op jit(solution)/shard_map/ppermute | solution.py:14
  104.1 296.4 %all-to-all-start.1 = ((bf16[8,1024,128]{2,0,1:T(8,128)(2,1)}), bf16[8,1024,128]{2,0,1:T(8,128)(2,1)}, u32[]{:S(2)}, u32[]{:S(2)}) async-start(bf16[8,1024,128]{2,0,1:T(8,128)(2,1)} %all-gather.3.cloned.1.call-done), calls=%async_computation.1 | async-start | bytes 4194304 | tf_op jit(solution)/shard_map/all_to_all | solution.py:66
  111.4 281.1 %all-reduce.2.cloned.1.call-start = ((), (), s32[]{:S(2)}) async-start(), calls=%async_computation.4 | async-start | bytes 8388608 | tf_op jit(solution)/shard_map/psum | solution.py:81
  127.0 65.9 %collective-permute-start.1 = (bf16[8,512,128]{2,1,0:T(8,128)(2,1)S(1)}, bf16[8,512,128]{2,1,0:T(8,128)(2,1)}, u32[]{:S(2)}, u32[]{:S(2)}) collective-permute-start(bf16[8,512,128]{2,1,0:T(8,128)(2,1)S(1)} %collective-permute-done), channel_id=1, source_target_pairs={{0,1},{1,2},{2,3},{3,4},{4,5},{5,6},{6,7},{7,0},{8,9},{9,10},{10,1... | collective-permute-start | bytes 3145736 | tf_op jit(solution)/shard_map/ppermute | solution.py:14
  132.2 64.1 %collective-permute-start.4 = (bf16[8,512,128]{2,1,0:T(8,128)(2,1)S(1)}, bf16[8,512,128]{2,1,0:T(8,128)(2,1)}, u32[]{:S(2)}, u32[]{:S(2)}) collective-permute-start(bf16[8,512,128]{2,1,0:T(8,128)(2,1)S(1)} %bitcast.40), channel_id=1, source_target_pairs={{0,7},{1,0},{2,1},{3,2},{4,3},{5,4},{6,5},{7,6},{8,15},{9,8},{10,9... | collective-permute-start | bytes 3145736 | tf_op jit(solution)/shard_map/ppermute | solution.py:16
  192.9 25.5 %collective-permute-start.2 = (bf16[8,512,128]{2,1,0:T(8,128)(2,1)}, bf16[8,512,128]{2,1,0:T(8,128)(2,1)}, u32[]{:S(2)}, u32[]{:S(2)}) collective-permute-start(bf16[8,512,128]{2,1,0:T(8,128)(2,1)} %collective-permute-done.1), channel_id=1, source_target_pairs={{0,1},{1,2},{2,3},{3,4},{4,5},{5,6},{6,7},{7,0},{8,9},{9,10},{10,1... | collective-permute-start | bytes 3145736 | tf_op jit(solution)/shard_map/ppermute | solution.py:14
  196.4 25.1 %collective-permute-start.5 = (bf16[8,512,128]{2,1,0:T(8,128)(2,1)}, bf16[8,512,128]{2,1,0:T(8,128)(2,1)}, u32[]{:S(2)}, u32[]{:S(2)}) collective-permute-start(bf16[8,512,128]{2,1,0:T(8,128)(2,1)} %collective-permute-done.4), channel_id=1, source_target_pairs={{0,7},{1,0},{2,1},{3,2},{4,3},{5,4},{6,5},{7,6},{8,15},{9,8},{10,9... | collective-permute-start | bytes 3145736 | tf_op jit(solution)/shard_map/ppermute | solution.py:16
  218.4 190.5 %collective-permute-start.3 = (bf16[8,512,128]{2,1,0:T(8,128)(2,1)}, bf16[8,512,128]{2,1,0:T(8,128)(2,1)}, u32[]{:S(2)}, u32[]{:S(2)}) collective-permute-start(bf16[8,512,128]{2,1,0:T(8,128)(2,1)} %collective-permute-done.2), channel_id=1, source_target_pairs={{0,1},{1,2},{2,3},{3,4},{4,5},{5,6},{6,7},{7,0},{8,9},{9,10},{10,1... | collective-permute-start | bytes 3145736 | tf_op jit(solution)/shard_map/ppermute | solution.py:14
  221.5 196.3 %collective-permute-start.6 = (bf16[8,512,128]{2,1,0:T(8,128)(2,1)}, bf16[8,512,128]{2,1,0:T(8,128)(2,1)}, u32[]{:S(2)}, u32[]{:S(2)}) collective-permute-start(bf16[8,512,128]{2,1,0:T(8,128)(2,1)} %collective-permute-done.5), channel_id=1, source_target_pairs={{0,7},{1,0},{2,1},{3,2},{4,3},{5,4},{6,5},{7,6},{8,15},{9,8},{10,9... | collective-permute-start | bytes 3145736 | tf_op jit(solution)/shard_map/ppermute | solution.py:16
  408.9 20.8 %copy-start.1 = (bf16[8,128,1024]{2,1,0:T(8,128)(2,1)S(1)}, bf16[8,128,1024]{2,1,0:T(8,128)(2,1)}, u32[]{:S(2)}) copy-start(bf16[8,128,1024]{2,1,0:T(8,128)(2,1)} %all_to_all.20) | copy-start | bytes 6291460
Sparse Core Ops, SparseCore 0:
  11.9 92.1 all-gather.2
  106.1 73.9 all-gather.4
  184.8 207.6 all-reduce.1
